TPU v7x, 32 devices: a whole 2x2x4 slice. The times are simulated.
32 devices in a mesh: groups: 2 (over y), fsdp: 4 (over x, core), tensor: 4 (over z).
Axes of the slice: x: 2, y: 2, z: 4, core: 2. Of those that a mesh axis runs over, the one named last changes fastest.
Arguments:
- tokens: bfloat16 [1024, 8192], P(('groups', 'fsdp')), parts along dimension 0, may hold values from -64 to 64
- gate_weight: bfloat16 [8192, 14336], P('fsdp', 'tensor'), may hold values from -0.0625 to 0.0625
- up_weight: bfloat16 [8192, 14336], P('fsdp', 'tensor'), may hold values from -0.0625 to 0.0625
- down_weight: bfloat16 [14336, 8192], P('tensor', 'fsdp'), may hold values from -0.046875 to 0.046875
- right_factor: bfloat16 [64, 128, 128], P('fsdp', 'tensor'), may hold values from -0.5 to 0.5
- left_factor: bfloat16 [128, 64, 64], P('fsdp', 'tensor'), may hold values from -0.75 to 0.75
Outputs:
- grad_right: float32 [128, 128, 128], P(('groups', 'fsdp'), 'tensor'), parts along dimension 0
- grad_left: float32 [256, 64, 64], P(('groups', 'fsdp'), 'tensor'), parts along dimension 0
There are 2 independent parts, one for each index of `groups`. A program takes and returns all parts, laid end to end along the dimension named above; an argument that names none is the same for every part. Nothing has to cross between parts.
All inputs are finite; a program needn't handle non-finite values.
Results may differ from a plain program's by a relative error of at most 0.0055.
Values may be sent and summed in bfloat16 or wider, within the bound.
A program may use at most 128 MiB of HBM per device.

v0:
```python
import math
import jax
import jax.numpy as jnp
from jax import lax
from jax.sharding import PartitionSpec as P


def body(tokens, gate_weight, up_weight, down_weight, right_factor, left_factor):
    fsdp_count = lax.axis_size("fsdp")
    tensor_count = lax.axis_size("tensor")
    tok_local = tokens.shape[0]
    group_rows = tok_local * fsdp_count
    share_rows = group_rows // tensor_count
    hid_local = gate_weight.shape[1]
    spread = lax.all_to_all(tokens, "fsdp", split_axis=1, concat_axis=0, tiled=True)
    student_in = lax.dynamic_slice_in_dim(
        spread, lax.axis_index("tensor") * share_rows, share_rows, 0
    )
    gate_part = jnp.dot(spread, gate_weight, preferred_element_type=jnp.float32)
    up_part = jnp.dot(spread, up_weight, preferred_element_type=jnp.float32)
    partial_value = jnp.concatenate([gate_part, up_part], axis=1)
    summed = lax.psum(partial_value.astype(jnp.bfloat16), "fsdp").astype(jnp.float32)
    hidden = (jax.nn.silu(summed[:, :hid_local]) * summed[:, hid_local:]).astype(jnp.bfloat16)
    target = lax.psum_scatter(
        jnp.dot(hidden, down_weight, preferred_element_type=jnp.float32).astype(jnp.bfloat16),
        "tensor",
        scatter_dimension=0,
        tiled=True,
    ).astype(jnp.float32)
    right_full, left_full = (
        lax.all_gather(right_factor, "tensor", axis=1, tiled=True),
        lax.all_gather(left_factor, "tensor", axis=1, tiled=True),
    )
    blocks_local = right_full.shape[0]
    block_size = right_full.shape[2]
    block_input = student_in.reshape(share_rows, blocks_local, block_size)
    mixed = jnp.einsum(
        "nij,ikj->nik", block_input, right_full, preferred_element_type=jnp.float32
    ).astype(jnp.bfloat16)
    routed = lax.all_to_all(mixed, "fsdp", split_axis=2, concat_axis=1, tiled=True)
    student = jnp.einsum("nij,jki->njk", routed, left_full, preferred_element_type=jnp.float32)
    inv_root = 1.0 / math.sqrt(group_rows)
    out_grad = (student - target.reshape(student.shape)) * inv_root
    grad_left = jnp.einsum("njk,nij->jki", out_grad, routed.astype(jnp.float32))
    mixed_grad = jnp.einsum("njk,jki->nij", out_grad, left_full.astype(jnp.float32)).astype(
        jnp.bfloat16
    )
    returned = lax.all_to_all(mixed_grad, "fsdp", split_axis=1, concat_axis=2, tiled=True)
    grad_right = jnp.einsum(
        "nik,nij->ikj", returned.astype(jnp.float32), block_input.astype(jnp.float32)
    )
    grad_right, grad_left = (
        lax.psum_scatter(grad_right, "tensor", scatter_dimension=1, tiled=True),
        lax.psum_scatter(grad_left, "tensor", scatter_dimension=1, tiled=True),
    )
    return (grad_right, grad_left)


def solution(mesh):
    return jax.shard_map(
        body,
        mesh=mesh,
        in_specs=(
            P(("groups", "fsdp"), None),
            P("fsdp", "tensor"),
            P("fsdp", "tensor"),
            P("tensor", "fsdp"),
            P("fsdp", "tensor", None),
            P("fsdp", "tensor", None),
        ),
        out_specs=(P(("groups", "fsdp"), "tensor", None), P(("groups", "fsdp"), "tensor", None)),
        check_vma=False,
    )
```

profile of v0, /device:TPU:0, one launch (start us, length us, event | category | flops | bytes accessed | tf_op | source)
XLA Modules:
  0.0 363.5 jit_solution(13968210217118573609)
XLA Ops:
  7.2 0.0 all-reduce.2.cloned.1.call-start
  7.2 4.1 %copy.27 = bf16[128,8192]{0,1:T(8,128)(2,1)} copy(bf16[128,8192]{1,0:T(8,128)(2,1)} %param.6) | data formatting | bytes 4194304 | tf_op args[0]
  11.3 29.9 %all_to_all.55 = bf16[128,4,2048]{0,2,1:T(8,128)(2,1)S(1)} all-to-all(bf16[128,4,2048]{0,2,1:T(8,128)(2,1)} %bitcast.39), channel_id=1, replica_groups=mesh['groups'=2,'fsdp'=4,'tensor'=4] {'fsdp'}, dimensions={1} | all-to-all | bytes 4194304 | tf_op jit(solution)/shard_map/all_to_all | solution.py:15
  41.2 2.6 copy.28
  43.8 0.0 copy-start
  43.8 13.7 %convolution_convert_fusion = bf16[512,3584]{1,0:T(8,128)(2,1)S(1)} fusion(bf16[512,2048]{1,0:T(8,128)(2,1)} %bitcast.45, bf16[2048,3584]{1,0:T(8,128)(2,1)} %param.8), kind=kOutput, calls=%fused_computation.3 | convolution fusion | flops 7518027776 | bytes 20447232 | tf_op jit(solution)/shard_map/dot_general | solution.py:20
  57.5 0.0 copy-done
  57.5 12.4 %convolution_convert_fusion.1 = bf16[512,3584]{1,0:T(8,128)(2,1)} fusion(bf16[512,2048]{1,0:T(8,128)(2,1)S(1)} %bitcast.47, bf16[2048,3584]{1,0:T(8,128)(2,1)} %param.7), kind=kOutput, calls=%fused_computation.4 | convolution fusion | flops 7518027776 | bytes 20447232 | tf_op jit(solution)/shard_map/dot_general | solution.py:19
  69.9 6.0 %pad_maximum_fusion = bf16[512,7168]{1,0:T(8,128)(2,1)} fusion(bf16[512,3584]{1,0:T(8,128)(2,1)S(1)} %convolution_convert_fusion, bf16[512,3584]{1,0:T(8,128)(2,1)} %convolution_convert_fusion.1), kind=kLoop, calls=%fused_computation.2 | loop fusion | flops 14680064 | bytes 14680064 | tf_op jit(solution)/shard_map/concatenate | solution.py:21
  75.9 0.0 all-reduce.2.cloned.1.call-update
  75.9 0.0 reduce-scatter.4.cloned.1.call-start
  76.0 137.9 %all-reduce.2.cloned.1.call-done = bf16[512,7168]{1,0:T(8,128)(2,1)} async-done(((bf16[512,7168]{1,0:T(8,128)(2,1)}), bf16[512,7168]{1,0:T(8,128)(2,1)}) %all-reduce.2.cloned.1.call-update) | async-done | bytes 7340048 | tf_op jit(solution)/shard_map/psum | solution.py:22
  213.9 10.2 %convert_element_type.29 = f32[512,7168]{1,0:T(8,128)} convert(bf16[512,7168]{1,0:T(8,128)(2,1)} %all-reduce.2.cloned.1.call-done) | non-fusion elementwise | flops 3670016 | bytes 22020096 | tf_op jit(solution)/shard_map/convert_element_type | solution.py:22
  224.1 0.0 copy-start.1
  224.1 16.5 %fusion.3 = bf16[512,2048]{1,0:T(8,128)(2,1)} fusion(bf16[3584,2048]{1,0:T(8,128)(2,1)} %param.9, f32[512,7168]{1,0:T(8,128)} %convert_element_type.29), kind=kOutput, calls=%fused_computation.6 | convolution fusion | flops 7528251392 | bytes 31457280 | tf_op jit(solution)/shard_map/dot_general | solution.py:25
  240.6 0.0 copy-start.2
  240.6 0.0 reduce-scatter.4.cloned.1.call-update
  240.6 0.0 copy-done.1
  240.6 22.3 %all_gather.6 = bf16[16,128,128]{2,1,0:T(8,128)(2,1)S(1)} all-gather(bf16[16,32,128]{2,1,0:T(8,128)(2,1)S(1)} %copy-done.1), channel_id=1, replica_groups=mesh['groups'=2,'fsdp'=4,'tensor'=4] {'tensor'}, dimensions={1}, use_global_device_ids=true | all-gather | bytes 655360 | tf_op jit(solution)/shard_map/all_gather | solution.py:31
  262.9 1.1 constant_dynamic-slice_fusion
  264.0 0.3 copy.29
  264.2 0.5 fusion.9
  264.8 1.2 copy.31
  266.0 3.5 all-to-all-start.1
  269.4 0.0 reduce-scatter.8.cloned.1.call-start
  269.5 0.0 copy-done.2
  269.5 22.2 %all_gather.7 = bf16[32,64,64]{2,1,0:T(8,128)(2,1)S(1)} all-gather(bf16[32,16,64]{2,1,0:T(8,128)(2,1)S(1)} %copy-done.2), channel_id=1, replica_groups=mesh['groups'=2,'fsdp'=4,'tensor'=4] {'tensor'}, dimensions={1}, use_global_device_ids=true | all-gather | bytes 327680 | tf_op jit(solution)/shard_map/all_gather | solution.py:32
  291.7 0.0 all-to-all-done.1
  291.7 0.1 copy.33
  291.7 6.0 %reduce-scatter.4.cloned.1.call-done = bf16[128,2048]{1,0:T(8,128)(2,1)} async-done(((bf16[512,2048]{1,0:T(8,128)(2,1)}), bf16[128,2048]{1,0:T(8,128)(2,1)}) %reduce-scatter.4.cloned.1.call-update) | async-done | bytes 524304 | tf_op jit(solution)/shard_map/reduce_scatter | solution.py:24
  297.7 1.2 copy.34
  299.0 0.3 fusion.7
  299.3 1.4 fusion.12
  300.7 0.0 reduce-scatter.8.cloned.1.call-update
  300.7 0.0 reduce-scatter.6.cloned.1.call-start
  300.8 0.3 fusion.8
  301.1 0.3 copy.35
  301.5 11.3 %all_to_all.56 = bf16[128,64,32]{0,2,1:T(8,128)(2,1)S(1)} all-to-all(bf16[128,64,32]{0,2,1:T(8,128)(2,1)S(1)} %copy.35), channel_id=1, replica_groups=mesh['groups'=2,'fsdp'=4,'tensor'=4] {'fsdp'}, dimensions={1} | all-to-all | bytes 1048576 | tf_op jit(solution)/shard_map/all_to_all | solution.py:48
  312.8 1.5 fusion.11
  314.3 0.0 reduce-scatter.6.cloned.1.call-update
  314.3 14.2 %reduce-scatter.8.cloned.1.call-done = f32[32,16,64]{2,1,0:T(8,128)} async-done(((f32[32,64,64]{2,1,0:T(8,128)}), f32[32,16,64]{2,1,0:T(8,128)}) %reduce-scatter.8.cloned.1.call-update) | async-done | bytes 131088 | tf_op jit(solution)/shard_map/reduce_scatter | solution.py:54
  328.5 28.5 %reduce-scatter.6.cloned.1.call-done = f32[16,32,128]{2,1,0:T(8,128)} async-done(((f32[16,128,128]{2,1,0:T(8,128)}), f32[16,32,128]{2,1,0:T(8,128)}) %reduce-scatter.6.cloned.1.call-update) | async-done | bytes 262160 | tf_op jit(solution)/shard_map/reduce_scatter | solution.py:53
  (1 shorter events, 0.0 us)
Async XLA Ops:
  7.2 206.7 %all-reduce.2.cloned.1.call-start = ((), (), s32[]{:S(2)}) async-start(), calls=%async_computation.6 | async-start | bytes 14680064 | tf_op jit(solution)/shard_map/psum | solution.py:22
  43.8 13.7 %copy-start = (bf16[4,128,2048]{2,1,0:T(8,128)(2,1)S(1)}, bf16[4,128,2048]{2,1,0:T(8,128)(2,1)}, u32[]{:S(2)}) copy-start(bf16[4,128,2048]{2,1,0:T(8,128)(2,1)} %copy.28) | copy-start | bytes 6291460
  75.9 221.8 %reduce-scatter.4.cloned.1.call-start = ((), (), s32[]{:S(2)}) async-start(), calls=%async_computation.7 | async-start | bytes 2621440 | tf_op jit(solution)/shard_map/reduce_scatter | solution.py:24
  224.1 16.6 %copy-start.1 = (bf16[16,32,128]{2,1,0:T(8,128)(2,1)S(1)}, bf16[16,32,128]{2,1,0:T(8,128)(2,1)}, u32[]{:S(2)}) copy-start(bf16[16,32,128]{2,1,0:T(8,128)(2,1)} %param.10) | copy-start | bytes 393220
  240.6 28.9 %copy-start.2 = (bf16[32,16,64]{2,1,0:T(8,128)(2,1)S(1)}, bf16[32,16,64]{2,1,0:T(8,128)(2,1)}, u32[]{:S(2)}) copy-start(bf16[32,16,64]{2,1,0:T(8,128)(2,1)} %param.11) | copy-start | bytes 196612
  266.0 25.7 %all-to-all-start.1 = ((bf16[128,16,128]{0,1,2:T(8,128)(2,1)}), bf16[128,16,128]{0,1,2:T(8,128)(2,1)S(1)}, u32[]{:S(2)}, u32[]{:S(2)}) async-start(bf16[128,16,128]{0,1,2:T(8,128)(2,1)} %copy.31), calls=%async_computation.1 | async-start | bytes 1048576 | tf_op jit(solution)/shard_map/all_to_all | solution.py:40
  269.4 59.0 %reduce-scatter.8.cloned.1.call-start = ((), (), s32[]{:S(2)}) async-start(), calls=%async_computation.9 | async-start | bytes 1310720 | tf_op jit(solution)/shard_map/reduce_scatter | solution.py:54
  300.7 56.3 %reduce-scatter.6.cloned.1.call-start = ((), (), s32[]{:S(2)}) async-start(), calls=%async_computation.8 | async-start | bytes 1310720 | tf_op jit(solution)/shard_map/reduce_scatter | solution.py:53
Sparse Core Ops, SparseCore 0:
  76.1 137.7 all-reduce.1
  240.7 56.9 reduce-scatter.3
  300.9 27.5 reduce-scatter.7
  331.2 25.7 reduce-scatter.5
where the time goes:
time: 364 us
  waiting for transfers between devices  187 us (51%)
  blocking collectives  85.6 us (24%)
  matrix products  46.6 us (13%)
  other arithmetic  16.2 us (4%)
  between operations  13.9 us (4%)
  local copies, waits for them, and re-layouts  11 us (3%)
  starting transfers between devices  3.64 us (1%)
    psum x1, waiting for transfers between devices, body(): lax.psum(partial_value.astype(jnp.bfloat16), 'fsdp').astype(jnp.float32)  138 us
    all_to_all x1, blocking collectives, body(): lax.all_to_all(tokens, 'fsdp', split_axis=1, concat_axis=0, tiled=True)  29.9 us
    reduce_scatter x1, waiting for transfers between devices, body(): lax.psum_scatter(grad_right, 'tensor', scatter_dimension=1, tiled=True)  28.5 us
    all_gather x1, blocking collectives, body(): lax.all_gather(right_factor, 'tensor', axis=1, tiled=True)  22.3 us
    all_gather x1, blocking collectives, body(): lax.all_gather(left_factor, 'tensor', axis=1, tiled=True)  22.2 us
    dot_general x1, matrix products, body(): jnp.dot(hidden, down_weight, preferred_element_type=jnp.float32)  16.5 us
    reduce_scatter x1, waiting for transfers between devices, body(): lax.psum_scatter(grad_left, 'tensor', scatter_dimension=1, tiled=True)  14.2 us
    dot_general x1, matrix products, body(): up_part = jnp.dot(spread, up_weight, preferred_element_type=jnp.float32)  13.7 us
  transfers between devices with their start and end apart: 5, of which 4 were waited for; matrix products, arithmetic and copies ran while one was open for 1% of the time, Pallas kernels for 0%

commit v1 on v0

--- a/solution.py
+++ b/solution.py
@@ -3,6 +3,12 @@
 import jax.numpy as jnp
 from jax import lax
 from jax.sharding import PartitionSpec as P
+
+
+def summed_here(x, name):
+    pieces = lax.all_gather(x, name, axis=0, tiled=False)
+    acc = pieces.sum(axis=0)
+    return acc
 
 
 def body(tokens, gate_weight, up_weight, down_weight, right_factor, left_factor):
@@ -19,7 +25,7 @@
     gate_part = jnp.dot(spread, gate_weight, preferred_element_type=jnp.float32)
     up_part = jnp.dot(spread, up_weight, preferred_element_type=jnp.float32)
     partial_value = jnp.concatenate([gate_part, up_part], axis=1)
-    summed = lax.psum(partial_value.astype(jnp.bfloat16), "fsdp").astype(jnp.float32)
+    summed = summed_here(partial_value.astype(jnp.bfloat16), "fsdp").astype(jnp.float32)
     hidden = (jax.nn.silu(summed[:, :hid_local]) * summed[:, hid_local:]).astype(jnp.bfloat16)
     target = lax.psum_scatter(
         jnp.dot(hidden, down_weight, preferred_element_type=jnp.float32).astype(jnp.bfloat16),

time: 364 us -> 420 us (1.15)
  waiting for transfers between devices: 187 us -> 228 us
  other arithmetic: 16.2 us -> 30.7 us
    all_gather x0 -> x1, waiting for transfers between devices: none -> 179 us  [summed_here(): pieces = lax.all_gather(x, name, axis=0, tiled=False)]
    psum x1 -> x0, waiting for transfers between devices: 138 us -> none  [body(): lax.psum(partial_value.astype(jnp.bfloat16), 'fsdp').astype(jnp.float32)]
    reduce_sum x0 -> x1, other arithmetic: none -> 14.9 us  [summed_here(): acc = pieces.sum(axis=0)]
where the time goes in v1:
time: 420 us; the launch traced here: 419 us
  waiting for transfers between devices  228 us (54%)
  blocking collectives  85.7 us (20%)
  matrix products  46.7 us (11%)
  other arithmetic  30.7 us (7%)
  between operations  13.9 us (3%)
  local copies, waits for them, and re-layouts  11 us (3%)
    all_gather x1, waiting for transfers between devices, summed_here(): pieces = lax.all_gather(x, name, axis=0, tiled=False)  179 us
    all_to_all x1, blocking collectives, body(): lax.all_to_all(tokens, 'fsdp', split_axis=1, concat_axis=0, tiled=True)  29.9 us
    reduce_scatter x1, waiting for transfers between devices, body(): lax.psum_scatter(grad_right, 'tensor', scatter_dimension=1, tiled=True)  28.5 us
    all_gather x1, blocking collectives, body(): lax.all_gather(left_factor, 'tensor', axis=1, tiled=True)  22.4 us
    all_gather x1, blocking collectives, body(): lax.all_gather(right_factor, 'tensor', axis=1, tiled=True)  22.1 us
    dot_general x1, matrix products, body(): jnp.dot(hidden, down_weight, preferred_element_type=jnp.float32)  16.5 us
    reduce_sum x1, other arithmetic, summed_here(): acc = pieces.sum(axis=0)  14.9 us
    dot_general x1, matrix products, body(): gate_part = jnp.dot(spread, gate_weight, preferred_element_type=jnp.float32)  13.8 us
  transfers between devices with their start and end apart: 5, of which 4 were waited for; matrix products, arithmetic and copies ran while one was open for 1% of the time, Pallas kernels for 0%

profile of v1, /device:TPU:0, one launch (start us, length us, event | category | flops | bytes accessed | tf_op | source)
XLA Modules:
  0.0 419.3 jit_solution(1726771100546967650)
XLA Ops:
  7.2 0.0 all-gather.2.cloned.1.call-start
  7.2 4.1 copy.27
  11.3 29.9 %all_to_all.55 = bf16[128,4,2048]{0,2,1:T(8,128)(2,1)S(1)} all-to-all(bf16[128,4,2048]{0,2,1:T(8,128)(2,1)} %bitcast.43), channel_id=1, replica_groups=mesh['groups'=2,'fsdp'=4,'tensor'=4] {'fsdp'}, dimensions={1} | all-to-all | bytes 4194304 | tf_op jit(solution)/shard_map/all_to_all | solution.py:21
  41.2 2.6 copy.28
  43.8 0.0 copy-start
  43.8 13.8 %fusion.1 = bf16[1,512,3584]{2,1,0:T(8,128)(2,1)S(1)} fusion(bf16[512,2048]{1,0:T(8,128)(2,1)} %bitcast.49, bf16[2048,3584]{1,0:T(8,128)(2,1)} %param.7), kind=kOutput, calls=%fused_computation.5 | convolution fusion | flops 7518027776 | bytes 20447232 | tf_op jit(solution)/shard_map/dot_general | solution.py:25
  57.6 0.0 copy-done
  57.6 12.4 %fusion.2 = bf16[1,512,3584]{2,1,0:T(8,128)(2,1)} fusion(bf16[512,2048]{1,0:T(8,128)(2,1)S(1)} %bitcast.51, bf16[2048,3584]{1,0:T(8,128)(2,1)} %param.8), kind=kOutput, calls=%fused_computation.6 | convolution fusion | flops 7518027776 | bytes 20447232 | tf_op jit(solution)/shard_map/dot_general | solution.py:26
  70.0 5.7 %pad_maximum_fusion = bf16[1,512,7168]{2,1,0:T(8,128)(2,1)} fusion(bf16[1,512,3584]{2,1,0:T(8,128)(2,1)} %fusion.2, bf16[1,512,3584]{2,1,0:T(8,128)(2,1)S(1)} %fusion.1), kind=kLoop, calls=%fused_computation.2 | loop fusion | flops 14680064 | bytes 14680064 | tf_op jit(solution)/shard_map/concatenate | solution.py:27
  75.7 0.0 all-gather.2.cloned.1.call-update
  75.7 0.2 reduce-scatter.4.cloned.1.call-start
  75.9 179.1 %all-gather.2.cloned.1.call-done = bf16[4,512,7168]{2,1,0:T(8,128)(2,1)} async-done(((bf16[1,512,7168]{2,1,0:T(8,128)(2,1)}), bf16[4,512,7168]{2,1,0:T(8,128)(2,1)}) %all-gather.2.cloned.1.call-update) | async-done | bytes 29360144 | tf_op jit(solution)/shard_map/all_gather | solution.py:9
  255.0 14.9 %reduce_sum.12 = bf16[512,7168]{1,0:T(8,128)(2,1)} reduce(bf16[4,512,7168]{2,1,0:T(8,128)(2,1)} %all-gather.2.cloned.1.call-done, bf16[]{:T(256)} %constant.6.clone.1), dimensions={0}, to_apply=%region_0.0 | reduce | flops 11010048 | bytes 36700160 | tf_op jit(solution)/shard_map/reduce_sum | solution.py:10
  269.9 10.2 %convert_element_type.38 = f32[512,7168]{1,0:T(8,128)} convert(bf16[512,7168]{1,0:T(8,128)(2,1)} %reduce_sum.12) | non-fusion elementwise | flops 3670016 | bytes 22020096 | tf_op jit(solution)/shard_map/convert_element_type | solution.py:28
  280.1 0.0 copy-start.1
  280.1 16.5 %fusion.5 = bf16[512,2048]{1,0:T(8,128)(2,1)} fusion(bf16[3584,2048]{1,0:T(8,128)(2,1)} %param.9, f32[512,7168]{1,0:T(8,128)} %convert_element_type.38), kind=kOutput, calls=%fused_computation.8 | convolution fusion | flops 7528251392 | bytes 31457280 | tf_op jit(solution)/shard_map/dot_general | solution.py:31
  296.6 0.0 copy-start.2
  296.6 0.0 reduce-scatter.4.cloned.1.call-update
  296.6 0.0 copy-done.1
  296.6 22.1 %all_gather.10 = bf16[16,128,128]{2,1,0:T(8,128)(2,1)S(1)} all-gather(bf16[16,32,128]{2,1,0:T(8,128)(2,1)S(1)} %copy-done.1), channel_id=1, replica_groups=mesh['groups'=2,'fsdp'=4,'tensor'=4] {'tensor'}, dimensions={1}, use_global_device_ids=true | all-gather | bytes 655360 | tf_op jit(solution)/shard_map/all_gather | solution.py:37
  318.8 1.1 constant_dynamic-slice_fusion
  319.8 0.3 copy.29
  320.1 0.5 fusion.11
  320.6 1.2 copy.31
  321.8 3.5 all-to-all-start.1
  325.3 0.0 reduce-scatter.8.cloned.1.call-start
  325.4 0.0 copy-done.2
  325.4 22.4 %all_gather.11 = bf16[32,64,64]{2,1,0:T(8,128)(2,1)S(1)} all-gather(bf16[32,16,64]{2,1,0:T(8,128)(2,1)S(1)} %copy-done.2), channel_id=1, replica_groups=mesh['groups'=2,'fsdp'=4,'tensor'=4] {'tensor'}, dimensions={1}, use_global_device_ids=true | all-gather | bytes 327680 | tf_op jit(solution)/shard_map/all_gather | solution.py:38
  347.8 0.0 all-to-all-done.1
  347.8 0.1 copy.33
  347.9 6.3 %reduce-scatter.4.cloned.1.call-done = bf16[128,2048]{1,0:T(8,128)(2,1)} async-done(((bf16[512,2048]{1,0:T(8,128)(2,1)}), bf16[128,2048]{1,0:T(8,128)(2,1)}) %reduce-scatter.4.cloned.1.call-update) | async-done | bytes 524304 | tf_op jit(solution)/shard_map/reduce_scatter | solution.py:30
  354.2 1.2 copy.34
  355.5 0.3 fusion.9
  355.7 1.4 fusion.14
  357.2 0.0 reduce-scatter.8.cloned.1.call-update
  357.2 0.0 reduce-scatter.6.cloned.1.call-start
  357.2 0.3 fusion.10
  357.6 0.3 copy.35
  357.9 11.2 %all_to_all.56 = bf16[128,64,32]{0,2,1:T(8,128)(2,1)S(1)} all-to-all(bf16[128,64,32]{0,2,1:T(8,128)(2,1)S(1)} %copy.35), channel_id=1, replica_groups=mesh['groups'=2,'fsdp'=4,'tensor'=4] {'fsdp'}, dimensions={1} | all-to-all | bytes 1048576 | tf_op jit(solution)/shard_map/all_to_all | solution.py:54
  369.2 1.5 fusion.13
  370.7 0.0 reduce-scatter.6.cloned.1.call-update
  370.7 13.5 %reduce-scatter.8.cloned.1.call-done = f32[32,16,64]{2,1,0:T(8,128)} async-done(((f32[32,64,64]{2,1,0:T(8,128)}), f32[32,16,64]{2,1,0:T(8,128)}) %reduce-scatter.8.cloned.1.call-update) | async-done | bytes 131088 | tf_op jit(solution)/shard_map/reduce_scatter | solution.py:60
  384.3 28.5 %reduce-scatter.6.cloned.1.call-done = f32[16,32,128]{2,1,0:T(8,128)} async-done(((f32[16,128,128]{2,1,0:T(8,128)}), f32[16,32,128]{2,1,0:T(8,128)}) %reduce-scatter.6.cloned.1.call-update) | async-done | bytes 262160 | tf_op jit(solution)/shard_map/reduce_scatter | solution.py:59
  (1 shorter events, 0.0 us)
Async XLA Ops:
  7.2 247.9 %all-gather.2.cloned.1.call-start = ((), (), s32[]{:S(2)}) async-start(), calls=%async_computation.6 | async-start | bytes 36700160 | tf_op jit(solution)/shard_map/all_gather | solution.py:9
  43.8 13.8 %copy-start = (bf16[4,128,2048]{2,1,0:T(8,128)(2,1)S(1)}, bf16[4,128,2048]{2,1,0:T(8,128)(2,1)}, u32[]{:S(2)}) copy-start(bf16[4,128,2048]{2,1,0:T(8,128)(2,1)} %copy.28) | copy-start | bytes 6291460
  75.7 278.5 %reduce-scatter.4.cloned.1.call-start = ((), (), s32[]{:S(2)}) async-start(), calls=%async_computation.7 | async-start | bytes 2621440 | tf_op jit(solution)/shard_map/reduce_scatter | solution.py:30
  280.1 16.6 %copy-start.1 = (bf16[16,32,128]{2,1,0:T(8,128)(2,1)S(1)}, bf16[16,32,128]{2,1,0:T(8,128)(2,1)}, u32[]{:S(2)}) copy-start(bf16[16,32,128]{2,1,0:T(8,128)(2,1)} %param.10) | copy-start | bytes 393220
  296.6 28.8 %copy-start.2 = (bf16[32,16,64]{2,1,0:T(8,128)(2,1)S(1)}, bf16[32,16,64]{2,1,0:T(8,128)(2,1)}, u32[]{:S(2)}) copy-start(bf16[32,16,64]{2,1,0:T(8,128)(2,1)} %param.11) | copy-start | bytes 196612
  321.8 26.0 %all-to-all-start.1 = ((bf16[128,16,128]{0,1,2:T(8,128)(2,1)}), bf16[128,16,128]{0,1,2:T(8,128)(2,1)S(1)}, u32[]{:S(2)}, u32[]{:S(2)}) async-start(bf16[128,16,128]{0,1,2:T(8,128)(2,1)} %copy.31), calls=%async_computation.1 | async-start | bytes 1048576 | tf_op jit(solution)/shard_map/all_to_all | solution.py:46
  325.3 59.0 %reduce-scatter.8.cloned.1.call-start = ((), (), s32[]{:S(2)}) async-start(), calls=%async_computation.9 | async-start | bytes 1310720 | tf_op jit(solution)/shard_map/reduce_scatter | solution.py:60
  357.2 55.6 %reduce-scatter.6.cloned.1.call-start = ((), (), s32[]{:S(2)}) async-start(), calls=%async_computation.8 | async-start | bytes 1310720 | tf_op jit(solution)/shard_map/reduce_scatter | solution.py:59
Sparse Core Ops, SparseCore 0:
  75.8 179.1 all-gather.1
  296.7 57.4 reduce-scatter.3
  357.3 26.8 reduce-scatter.7
  387.0 25.7 reduce-scatter.5
